TPU v7x, 512 devices: a whole 4x8x8 slice. The times are simulated.
512 devices in a mesh: slab: 16 (over z, core), cross: 32 (over y, x).
Axes of the slice: x: 4, y: 8, z: 8, core: 2. Of those that a mesh axis runs over, the one named last changes fastest.
Arguments:
- thickness: int32 [16], P('slab'), may hold values from 1 to 4, as said below
- layer_sources: bfloat16 [64, 128, 32768], P('slab', None, 'cross'), may hold values from -6 to 6
- green_down: bfloat16 [16, 1536, 128, 128], P('slab', 'cross'), may hold values from -0.1875 to 0.1875
- column_down: int32 [16, 1536], P('slab', 'cross'), may hold values from 0 to 255, as said below
- green_up: bfloat16 [16, 1536, 128, 128], P('slab', 'cross'), may hold values from -0.1875 to 0.1875
- column_up: int32 [16, 1536], P('slab', 'cross'), may hold values from 0 to 255, as said below
Outputs:
- down_traces: bfloat16 [16, 128, 32768], P('slab', None, 'cross')
- up_traces: bfloat16 [16, 128, 32768], P('slab', None, 'cross')
Inputs may be any that keep to these rules, and one draw needn't show every extreme that they name: `thickness`: each slab has 1 to 4 layers; some slab has exactly 4 and another exactly 1. `column_down`: the 6 columns of block row i are distinct, each equals (i + o) modulo 256 for some o with -4 <= o <= 4, and they include (i + 4) modulo 256. `column_up`: as for column_down.
All inputs are finite; a program needn't handle non-finite values.
Results may differ from a plain program's by a relative error of at most 0.015.
Values may be sent and summed in bfloat16 or wider, within the bound.
A program may use at most 64 MiB of HBM per device.

v0:
```python
import jax
import jax.numpy as jnp
from jax import lax
from jax.sharding import PartitionSpec as P

HB = 4
MB = 4
BM = 32


def padded(cells, sides, width):
    for axis, dim in sides:
        count = lax.axis_size(axis)
        head = lax.slice_in_dim(cells, 0, width, axis=dim)
        tail = lax.slice_in_dim(cells, cells.shape[dim] - width, cells.shape[dim], axis=dim)
        cells = jnp.concatenate(
            [
                lax.ppermute(tail, axis, [(i, (i + 1) % count) for i in range(count)]),
                cells,
                lax.ppermute(head, axis, [((i + 1) % count, i) for i in range(count)]),
            ],
            axis=dim,
        )
    return cells


def passed_along(block, axis, distance):
    devices = range(lax.axis_size(axis))
    route = [(i - distance, i) for i in devices if i - distance in devices]
    return lax.ppermute(block, axis, route)


def shards(thickness, layer_sources, green_down, column_down, green_up, column_up):
    slabs = lax.axis_size("slab")
    slab_id = lax.axis_index("slab")
    lateral = lax.axis_index("cross")
    depth = layer_sources.shape[0]
    width = layer_sources.shape[2]
    bsize = green_down.shape[-1]
    per_dev = width // bsize
    total_blocks = per_dev * lax.axis_size("cross")
    kcount = green_down.shape[1] // per_dev
    keep = (jnp.arange(depth) < thickness[0]).astype(jnp.float32)
    source = jnp.sum(layer_sources.astype(jnp.float32) * keep[:, None, None], axis=0)
    group = 1
    rows = BM * group
    groups = MB // group
    steps = slabs + groups - 1
    local_down = (column_down[0] - lateral * per_dev + HB) % total_blocks
    local_up = (column_up[0] - lateral * per_dev + HB) % total_blocks

    def product(extended, blocks, local_cols):
        tiles = extended.reshape(rows, per_dev + 2 * HB, bsize)
        picked = jnp.take(tiles, local_cols, axis=1)
        prod = jnp.einsum("mnb,nab->mna", picked, blocks, preferred_element_type=jnp.float32)
        return prod.reshape(rows, per_dev, kcount, bsize).sum(axis=2).reshape(rows, width)

    def finish(extended, blocks, local_cols, which, stored):
        active = jnp.logical_and(which >= 0, which < groups)
        start = jnp.clip(which, 0, groups - 1) * rows
        added = lax.dynamic_slice_in_dim(source, start, rows, 0)
        result = (product(extended, blocks, local_cols) + added).astype(jnp.bfloat16)
        current = lax.dynamic_slice_in_dim(stored, start, rows, 0)
        stored = lax.dynamic_update_slice_in_dim(
            stored, jnp.where(active, result, current), start, 0
        )
        return (result, stored)

    def one_step(step, carry):
        incoming_down, incoming_up, stored_down, stored_up = carry
        ext_down = padded(incoming_down, (("cross", 1),), HB * bsize)
        ext_up = padded(incoming_up, (("cross", 1),), HB * bsize)
        result_down, stored_down = finish(
            ext_down, green_down[0], local_down, step - slab_id, stored_down
        )
        result_up, stored_up = finish(
            ext_up, green_up[0], local_up, step - (slabs - 1 - slab_id), stored_up
        )
        incoming_down = passed_along(result_down, "slab", 1)
        incoming_up = passed_along(result_up, "slab", -1)
        return (incoming_down, incoming_up, stored_down, stored_up)

    empty = jnp.zeros((rows, width), jnp.bfloat16)
    stored = jnp.zeros((layer_sources.shape[1], width), jnp.bfloat16)
    final = lax.fori_loop(0, steps, one_step, (empty, empty, stored, stored))
    return (final[2][None], final[3][None])


def solution(mesh):
    return jax.shard_map(
        shards,
        mesh=mesh,
        in_specs=(
            P("slab"),
            P("slab", None, "cross"),
            P("slab", "cross", None, None),
            P("slab", "cross"),
            P("slab", "cross", None, None),
            P("slab", "cross"),
        ),
        out_specs=(P("slab", None, "cross"), P("slab", None, "cross")),
        check_vma=False,
    )
```

profile of v0, /device:TPU:193, one launch (start us, length us, event | category | flops | bytes accessed | tf_op | source)
XLA Modules:
  0.0 651.2 jit_solution(2056670101882679880)
XLA Ops:
  5.2 646.1 %while.20 = (s32[]{:T(128)}, bf16[32,1024]{1,0:T(8,128)(2,1)S(1)}, bf16[32,1024]{1,0:T(8,128)(2,1)S(1)}, bf16[128,1024]{1,0:T(8,128)(2,1)}, bf16[128,1024]{1,0:T...) while((s32[]{:T(128)}, bf16[32,1024]{1,0:T(8,128)(2,1)S(1)}, ...), condition=%wide.region_4.6_spmd, body=%wide.region_1.5_spmd.sunk | while | flops 102370160 | bytes 11676349 | solution.py:85
  5.2 7.3 %collective-permute-start.2 = (bf16[32,512]{1,0:T(8,128)(2,1)S(1)}, bf16[32,512]{1,0:T(8,128)(2,1)S(1)}, u32[]{:S(2)}, u32[]{:S(2)}) collective-permute-start(bf16[32,512]{1,0:T(8,128)(2,1)S(1)} %get-tuple-element.368), channel_id=1, source_target_pairs={{1,0},{2,1},{3,2},{4,3},{5,4},{6,5},{7,6},{8,7},{9,8},{10,9},{11,1... | collective-permute-start | bytes 98312 | tf_op jit(solution)/shard_map/while/body/eval_jaxpr/ppermute | solution.py:20
  14.4 6.7 %collective-permute-start = (bf16[32,512]{1,0:T(8,128)(2,1)S(1)}, bf16[32,512]{1,0:T(8,128)(2,1)S(1)}, u32[]{:S(2)}, u32[]{:S(2)}) collective-permute-start(bf16[32,512]{1,0:T(8,128)(2,1)S(1)} %get-tuple-element.364), channel_id=1, source_target_pairs={{1,0},{2,1},{3,2},{4,3},{5,4},{6,5},{7,6},{8,7},{9,8},{10,9},{11,1... | collective-permute-start | bytes 98312 | tf_op jit(solution)/shard_map/while/body/eval_jaxpr/ppermute | solution.py:20
  32.4 7.7 %collective-permute-start.4 = (bf16[32,1024]{1,0:T(8,128)(2,1)S(1)}, bf16[32,1024]{1,0:T(8,128)(2,1)S(1)}, u32[]{:S(2)}, u32[]{:S(2)}) collective-permute-start(bf16[32,1024]{1,0:T(8,128)(2,1)S(1)} %get-tuple-element.372), channel_id=1, source_target_pairs={{0,32},{32,64},{64,96},{96,128},{128,160},{160,192},{192,224},{224... | collective-permute-start | bytes 196616 | tf_op jit(solution)/shard_map/while/body/eval_jaxpr/ppermute | solution.py:30
  52.2 6.3 collective-permute-start
  75.7 4.9 collective-permute-done.5
  85.8 6.3 collective-permute-start
  119.4 6.3 collective-permute-start
  153.0 6.3 collective-permute-start
  176.4 4.9 collective-permute-done.5
  186.5 6.3 collective-permute-start
  209.9 4.9 collective-permute-done.5
  220.1 6.3 collective-permute-start
  253.7 6.3 collective-permute-start
  277.1 4.9 collective-permute-done.5
  287.2 6.3 collective-permute-start
  310.7 4.9 collective-permute-done.5
  320.8 6.3 collective-permute-start
  354.4 6.3 collective-permute-start
  377.8 4.9 collective-permute-done.5
  388.0 6.3 collective-permute-start
  411.4 4.9 collective-permute-done.5
  421.5 6.3 collective-permute-start
  455.1 6.3 collective-permute-start
  478.5 4.9 collective-permute-done.5
  488.7 6.3 collective-permute-start
  512.1 4.9 collective-permute-done.5
  522.2 6.3 collective-permute-start
  555.8 6.3 collective-permute-start
  579.2 4.9 collective-permute-done.5
  589.4 6.3 collective-permute-start
  622.9 6.3 collective-permute-start
  (491 shorter events, 461.8 us)
Async XLA Ops:
  5.2 18.0 %collective-permute-start.2 = (bf16[32,512]{1,0:T(8,128)(2,1)S(1)}, bf16[32,512]{1,0:T(8,128)(2,1)S(1)}, u32[]{:S(2)}, u32[]{:S(2)}) collective-permute-start(bf16[32,512]{1,0:T(8,128)(2,1)S(1)} %get-tuple-element.368), channel_id=1, source_target_pairs={{1,0},{2,1},{3,2},{4,3},{5,4},{6,5},{7,6},{8,7},{9,8},{10,9},{11,1... | collective-permute-start | bytes 98312 | tf_op jit(solution)/shard_map/while/body/eval_jaxpr/ppermute | solution.py:20
  14.4 11.8 %collective-permute-start = (bf16[32,512]{1,0:T(8,128)(2,1)S(1)}, bf16[32,512]{1,0:T(8,128)(2,1)S(1)}, u32[]{:S(2)}, u32[]{:S(2)}) collective-permute-start(bf16[32,512]{1,0:T(8,128)(2,1)S(1)} %get-tuple-element.364), channel_id=1, source_target_pairs={{1,0},{2,1},{3,2},{4,3},{5,4},{6,5},{7,6},{8,7},{9,8},{10,9},{11,1... | collective-permute-start | bytes 98312 | tf_op jit(solution)/shard_map/while/body/eval_jaxpr/ppermute | solution.py:20
  46.9 13.7 %collective-permute-start.2 = (bf16[32,512]{1,0:T(8,128)(2,1)S(1)}, bf16[32,512]{1,0:T(8,128)(2,1)S(1)}, u32[]{:S(2)}, u32[]{:S(2)}) collective-permute-start(bf16[32,512]{1,0:T(8,128)(2,1)S(1)} %get-tuple-element.368), channel_id=1, source_target_pairs={{1,0},{2,1},{3,2},{4,3},{5,4},{6,5},{7,6},{8,7},{9,8},{10,9},{11,1... | collective-permute-start | bytes 98312 | tf_op jit(solution)/shard_map/while/body/eval_jaxpr/ppermute | solution.py:20
  52.2 11.5 %collective-permute-start = (bf16[32,512]{1,0:T(8,128)(2,1)S(1)}, bf16[32,512]{1,0:T(8,128)(2,1)S(1)}, u32[]{:S(2)}, u32[]{:S(2)}) collective-permute-start(bf16[32,512]{1,0:T(8,128)(2,1)S(1)} %get-tuple-element.364), channel_id=1, source_target_pairs={{1,0},{2,1},{3,2},{4,3},{5,4},{6,5},{7,6},{8,7},{9,8},{10,9},{11,1... | collective-permute-start | bytes 98312 | tf_op jit(solution)/shard_map/while/body/eval_jaxpr/ppermute | solution.py:20
  80.5 13.7 %collective-permute-start.2 = (bf16[32,512]{1,0:T(8,128)(2,1)S(1)}, bf16[32,512]{1,0:T(8,128)(2,1)S(1)}, u32[]{:S(2)}, u32[]{:S(2)}) collective-permute-start(bf16[32,512]{1,0:T(8,128)(2,1)S(1)} %get-tuple-element.368), channel_id=1, source_target_pairs={{1,0},{2,1},{3,2},{4,3},{5,4},{6,5},{7,6},{8,7},{9,8},{10,9},{11,1... | collective-permute-start | bytes 98312 | tf_op jit(solution)/shard_map/while/body/eval_jaxpr/ppermute | solution.py:20
  85.8 11.5 %collective-permute-start = (bf16[32,512]{1,0:T(8,128)(2,1)S(1)}, bf16[32,512]{1,0:T(8,128)(2,1)S(1)}, u32[]{:S(2)}, u32[]{:S(2)}) collective-permute-start(bf16[32,512]{1,0:T(8,128)(2,1)S(1)} %get-tuple-element.364), channel_id=1, source_target_pairs={{1,0},{2,1},{3,2},{4,3},{5,4},{6,5},{7,6},{8,7},{9,8},{10,9},{11,1... | collective-permute-start | bytes 98312 | tf_op jit(solution)/shard_map/while/body/eval_jaxpr/ppermute | solution.py:20
  114.1 13.7 %collective-permute-start.2 = (bf16[32,512]{1,0:T(8,128)(2,1)S(1)}, bf16[32,512]{1,0:T(8,128)(2,1)S(1)}, u32[]{:S(2)}, u32[]{:S(2)}) collective-permute-start(bf16[32,512]{1,0:T(8,128)(2,1)S(1)} %get-tuple-element.368), channel_id=1, source_target_pairs={{1,0},{2,1},{3,2},{4,3},{5,4},{6,5},{7,6},{8,7},{9,8},{10,9},{11,1... | collective-permute-start | bytes 98312 | tf_op jit(solution)/shard_map/while/body/eval_jaxpr/ppermute | solution.py:20
  119.4 11.5 %collective-permute-start = (bf16[32,512]{1,0:T(8,128)(2,1)S(1)}, bf16[32,512]{1,0:T(8,128)(2,1)S(1)}, u32[]{:S(2)}, u32[]{:S(2)}) collective-permute-start(bf16[32,512]{1,0:T(8,128)(2,1)S(1)} %get-tuple-element.364), channel_id=1, source_target_pairs={{1,0},{2,1},{3,2},{4,3},{5,4},{6,5},{7,6},{8,7},{9,8},{10,9},{11,1... | collective-permute-start | bytes 98312 | tf_op jit(solution)/shard_map/while/body/eval_jaxpr/ppermute | solution.py:20
  147.7 13.7 %collective-permute-start.2 = (bf16[32,512]{1,0:T(8,128)(2,1)S(1)}, bf16[32,512]{1,0:T(8,128)(2,1)S(1)}, u32[]{:S(2)}, u32[]{:S(2)}) collective-permute-start(bf16[32,512]{1,0:T(8,128)(2,1)S(1)} %get-tuple-element.368), channel_id=1, source_target_pairs={{1,0},{2,1},{3,2},{4,3},{5,4},{6,5},{7,6},{8,7},{9,8},{10,9},{11,1... | collective-permute-start | bytes 98312 | tf_op jit(solution)/shard_map/while/body/eval_jaxpr/ppermute | solution.py:20
  153.0 11.5 %collective-permute-start = (bf16[32,512]{1,0:T(8,128)(2,1)S(1)}, bf16[32,512]{1,0:T(8,128)(2,1)S(1)}, u32[]{:S(2)}, u32[]{:S(2)}) collective-permute-start(bf16[32,512]{1,0:T(8,128)(2,1)S(1)} %get-tuple-element.364), channel_id=1, source_target_pairs={{1,0},{2,1},{3,2},{4,3},{5,4},{6,5},{7,6},{8,7},{9,8},{10,9},{11,1... | collective-permute-start | bytes 98312 | tf_op jit(solution)/shard_map/while/body/eval_jaxpr/ppermute | solution.py:20
  181.2 13.7 %collective-permute-start.2 = (bf16[32,512]{1,0:T(8,128)(2,1)S(1)}, bf16[32,512]{1,0:T(8,128)(2,1)S(1)}, u32[]{:S(2)}, u32[]{:S(2)}) collective-permute-start(bf16[32,512]{1,0:T(8,128)(2,1)S(1)} %get-tuple-element.368), channel_id=1, source_target_pairs={{1,0},{2,1},{3,2},{4,3},{5,4},{6,5},{7,6},{8,7},{9,8},{10,9},{11,1... | collective-permute-start | bytes 98312 | tf_op jit(solution)/shard_map/while/body/eval_jaxpr/ppermute | solution.py:20
  186.5 11.5 %collective-permute-start = (bf16[32,512]{1,0:T(8,128)(2,1)S(1)}, bf16[32,512]{1,0:T(8,128)(2,1)S(1)}, u32[]{:S(2)}, u32[]{:S(2)}) collective-permute-start(bf16[32,512]{1,0:T(8,128)(2,1)S(1)} %get-tuple-element.364), channel_id=1, source_target_pairs={{1,0},{2,1},{3,2},{4,3},{5,4},{6,5},{7,6},{8,7},{9,8},{10,9},{11,1... | collective-permute-start | bytes 98312 | tf_op jit(solution)/shard_map/while/body/eval_jaxpr/ppermute | solution.py:20
  214.8 13.7 %collective-permute-start.2 = (bf16[32,512]{1,0:T(8,128)(2,1)S(1)}, bf16[32,512]{1,0:T(8,128)(2,1)S(1)}, u32[]{:S(2)}, u32[]{:S(2)}) collective-permute-start(bf16[32,512]{1,0:T(8,128)(2,1)S(1)} %get-tuple-element.368), channel_id=1, source_target_pairs={{1,0},{2,1},{3,2},{4,3},{5,4},{6,5},{7,6},{8,7},{9,8},{10,9},{11,1... | collective-permute-start | bytes 98312 | tf_op jit(solution)/shard_map/while/body/eval_jaxpr/ppermute | solution.py:20
  248.4 13.7 %collective-permute-start.2 = (bf16[32,512]{1,0:T(8,128)(2,1)S(1)}, bf16[32,512]{1,0:T(8,128)(2,1)S(1)}, u32[]{:S(2)}, u32[]{:S(2)}) collective-permute-start(bf16[32,512]{1,0:T(8,128)(2,1)S(1)} %get-tuple-element.368), channel_id=1, source_target_pairs={{1,0},{2,1},{3,2},{4,3},{5,4},{6,5},{7,6},{8,7},{9,8},{10,9},{11,1... | collective-permute-start | bytes 98312 | tf_op jit(solution)/shard_map/while/body/eval_jaxpr/ppermute | solution.py:20
  253.7 11.5 %collective-permute-start = (bf16[32,512]{1,0:T(8,128)(2,1)S(1)}, bf16[32,512]{1,0:T(8,128)(2,1)S(1)}, u32[]{:S(2)}, u32[]{:S(2)}) collective-permute-start(bf16[32,512]{1,0:T(8,128)(2,1)S(1)} %get-tuple-element.364), channel_id=1, source_target_pairs={{1,0},{2,1},{3,2},{4,3},{5,4},{6,5},{7,6},{8,7},{9,8},{10,9},{11,1... | collective-permute-start | bytes 98312 | tf_op jit(solution)/shard_map/while/body/eval_jaxpr/ppermute | solution.py:20
  281.9 13.7 %collective-permute-start.2 = (bf16[32,512]{1,0:T(8,128)(2,1)S(1)}, bf16[32,512]{1,0:T(8,128)(2,1)S(1)}, u32[]{:S(2)}, u32[]{:S(2)}) collective-permute-start(bf16[32,512]{1,0:T(8,128)(2,1)S(1)} %get-tuple-element.368), channel_id=1, source_target_pairs={{1,0},{2,1},{3,2},{4,3},{5,4},{6,5},{7,6},{8,7},{9,8},{10,9},{11,1... | collective-permute-start | bytes 98312 | tf_op jit(solution)/shard_map/while/body/eval_jaxpr/ppermute | solution.py:20
  287.2 11.5 %collective-permute-start = (bf16[32,512]{1,0:T(8,128)(2,1)S(1)}, bf16[32,512]{1,0:T(8,128)(2,1)S(1)}, u32[]{:S(2)}, u32[]{:S(2)}) collective-permute-start(bf16[32,512]{1,0:T(8,128)(2,1)S(1)} %get-tuple-element.364), channel_id=1, source_target_pairs={{1,0},{2,1},{3,2},{4,3},{5,4},{6,5},{7,6},{8,7},{9,8},{10,9},{11,1... | collective-permute-start | bytes 98312 | tf_op jit(solution)/shard_map/while/body/eval_jaxpr/ppermute | solution.py:20
  315.5 13.7 %collective-permute-start.2 = (bf16[32,512]{1,0:T(8,128)(2,1)S(1)}, bf16[32,512]{1,0:T(8,128)(2,1)S(1)}, u32[]{:S(2)}, u32[]{:S(2)}) collective-permute-start(bf16[32,512]{1,0:T(8,128)(2,1)S(1)} %get-tuple-element.368), channel_id=1, source_target_pairs={{1,0},{2,1},{3,2},{4,3},{5,4},{6,5},{7,6},{8,7},{9,8},{10,9},{11,1... | collective-permute-start | bytes 98312 | tf_op jit(solution)/shard_map/while/body/eval_jaxpr/ppermute | solution.py:20
  349.1 13.7 %collective-permute-start.2 = (bf16[32,512]{1,0:T(8,128)(2,1)S(1)}, bf16[32,512]{1,0:T(8,128)(2,1)S(1)}, u32[]{:S(2)}, u32[]{:S(2)}) collective-permute-start(bf16[32,512]{1,0:T(8,128)(2,1)S(1)} %get-tuple-element.368), channel_id=1, source_target_pairs={{1,0},{2,1},{3,2},{4,3},{5,4},{6,5},{7,6},{8,7},{9,8},{10,9},{11,1... | collective-permute-start | bytes 98312 | tf_op jit(solution)/shard_map/while/body/eval_jaxpr/ppermute | solution.py:20
  354.4 11.5 %collective-permute-start = (bf16[32,512]{1,0:T(8,128)(2,1)S(1)}, bf16[32,512]{1,0:T(8,128)(2,1)S(1)}, u32[]{:S(2)}, u32[]{:S(2)}) collective-permute-start(bf16[32,512]{1,0:T(8,128)(2,1)S(1)} %get-tuple-element.364), channel_id=1, source_target_pairs={{1,0},{2,1},{3,2},{4,3},{5,4},{6,5},{7,6},{8,7},{9,8},{10,9},{11,1... | collective-permute-start | bytes 98312 | tf_op jit(solution)/shard_map/while/body/eval_jaxpr/ppermute | solution.py:20
  382.7 13.7 %collective-permute-start.2 = (bf16[32,512]{1,0:T(8,128)(2,1)S(1)}, bf16[32,512]{1,0:T(8,128)(2,1)S(1)}, u32[]{:S(2)}, u32[]{:S(2)}) collective-permute-start(bf16[32,512]{1,0:T(8,128)(2,1)S(1)} %get-tuple-element.368), channel_id=1, source_target_pairs={{1,0},{2,1},{3,2},{4,3},{5,4},{6,5},{7,6},{8,7},{9,8},{10,9},{11,1... | collective-permute-start | bytes 98312 | tf_op jit(solution)/shard_map/while/body/eval_jaxpr/ppermute | solution.py:20
  388.0 11.5 %collective-permute-start = (bf16[32,512]{1,0:T(8,128)(2,1)S(1)}, bf16[32,512]{1,0:T(8,128)(2,1)S(1)}, u32[]{:S(2)}, u32[]{:S(2)}) collective-permute-start(bf16[32,512]{1,0:T(8,128)(2,1)S(1)} %get-tuple-element.364), channel_id=1, source_target_pairs={{1,0},{2,1},{3,2},{4,3},{5,4},{6,5},{7,6},{8,7},{9,8},{10,9},{11,1... | collective-permute-start | bytes 98312 | tf_op jit(solution)/shard_map/while/body/eval_jaxpr/ppermute | solution.py:20
  416.2 13.7 %collective-permute-start.2 = (bf16[32,512]{1,0:T(8,128)(2,1)S(1)}, bf16[32,512]{1,0:T(8,128)(2,1)S(1)}, u32[]{:S(2)}, u32[]{:S(2)}) collective-permute-start(bf16[32,512]{1,0:T(8,128)(2,1)S(1)} %get-tuple-element.368), channel_id=1, source_target_pairs={{1,0},{2,1},{3,2},{4,3},{5,4},{6,5},{7,6},{8,7},{9,8},{10,9},{11,1... | collective-permute-start | bytes 98312 | tf_op jit(solution)/shard_map/while/body/eval_jaxpr/ppermute | solution.py:20
  449.8 13.7 %collective-permute-start.2 = (bf16[32,512]{1,0:T(8,128)(2,1)S(1)}, bf16[32,512]{1,0:T(8,128)(2,1)S(1)}, u32[]{:S(2)}, u32[]{:S(2)}) collective-permute-start(bf16[32,512]{1,0:T(8,128)(2,1)S(1)} %get-tuple-element.368), channel_id=1, source_target_pairs={{1,0},{2,1},{3,2},{4,3},{5,4},{6,5},{7,6},{8,7},{9,8},{10,9},{11,1... | collective-permute-start | bytes 98312 | tf_op jit(solution)/shard_map/while/body/eval_jaxpr/ppermute | solution.py:20
  455.1 11.5 %collective-permute-start = (bf16[32,512]{1,0:T(8,128)(2,1)S(1)}, bf16[32,512]{1,0:T(8,128)(2,1)S(1)}, u32[]{:S(2)}, u32[]{:S(2)}) collective-permute-start(bf16[32,512]{1,0:T(8,128)(2,1)S(1)} %get-tuple-element.364), channel_id=1, source_target_pairs={{1,0},{2,1},{3,2},{4,3},{5,4},{6,5},{7,6},{8,7},{9,8},{10,9},{11,1... | collective-permute-start | bytes 98312 | tf_op jit(solution)/shard_map/while/body/eval_jaxpr/ppermute | solution.py:20
  483.4 13.7 %collective-permute-start.2 = (bf16[32,512]{1,0:T(8,128)(2,1)S(1)}, bf16[32,512]{1,0:T(8,128)(2,1)S(1)}, u32[]{:S(2)}, u32[]{:S(2)}) collective-permute-start(bf16[32,512]{1,0:T(8,128)(2,1)S(1)} %get-tuple-element.368), channel_id=1, source_target_pairs={{1,0},{2,1},{3,2},{4,3},{5,4},{6,5},{7,6},{8,7},{9,8},{10,9},{11,1... | collective-permute-start | bytes 98312 | tf_op jit(solution)/shard_map/while/body/eval_jaxpr/ppermute | solution.py:20
  488.7 11.5 %collective-permute-start = (bf16[32,512]{1,0:T(8,128)(2,1)S(1)}, bf16[32,512]{1,0:T(8,128)(2,1)S(1)}, u32[]{:S(2)}, u32[]{:S(2)}) collective-permute-start(bf16[32,512]{1,0:T(8,128)(2,1)S(1)} %get-tuple-element.364), channel_id=1, source_target_pairs={{1,0},{2,1},{3,2},{4,3},{5,4},{6,5},{7,6},{8,7},{9,8},{10,9},{11,1... | collective-permute-start | bytes 98312 | tf_op jit(solution)/shard_map/while/body/eval_jaxpr/ppermute | solution.py:20
  516.9 13.7 %collective-permute-start.2 = (bf16[32,512]{1,0:T(8,128)(2,1)S(1)}, bf16[32,512]{1,0:T(8,128)(2,1)S(1)}, u32[]{:S(2)}, u32[]{:S(2)}) collective-permute-start(bf16[32,512]{1,0:T(8,128)(2,1)S(1)} %get-tuple-element.368), channel_id=1, source_target_pairs={{1,0},{2,1},{3,2},{4,3},{5,4},{6,5},{7,6},{8,7},{9,8},{10,9},{11,1... | collective-permute-start | bytes 98312 | tf_op jit(solution)/shard_map/while/body/eval_jaxpr/ppermute | solution.py:20
  550.5 13.7 %collective-permute-start.2 = (bf16[32,512]{1,0:T(8,128)(2,1)S(1)}, bf16[32,512]{1,0:T(8,128)(2,1)S(1)}, u32[]{:S(2)}, u32[]{:S(2)}) collective-permute-start(bf16[32,512]{1,0:T(8,128)(2,1)S(1)} %get-tuple-element.368), channel_id=1, source_target_pairs={{1,0},{2,1},{3,2},{4,3},{5,4},{6,5},{7,6},{8,7},{9,8},{10,9},{11,1... | collective-permute-start | bytes 98312 | tf_op jit(solution)/shard_map/while/body/eval_jaxpr/ppermute | solution.py:20
  584.1 13.7 %collective-permute-start.2 = (bf16[32,512]{1,0:T(8,128)(2,1)S(1)}, bf16[32,512]{1,0:T(8,128)(2,1)S(1)}, u32[]{:S(2)}, u32[]{:S(2)}) collective-permute-start(bf16[32,512]{1,0:T(8,128)(2,1)S(1)} %get-tuple-element.368), channel_id=1, source_target_pairs={{1,0},{2,1},{3,2},{4,3},{5,4},{6,5},{7,6},{8,7},{9,8},{10,9},{11,1... | collective-permute-start | bytes 98312 | tf_op jit(solution)/shard_map/while/body/eval_jaxpr/ppermute | solution.py:20
  589.4 11.5 %collective-permute-start = (bf16[32,512]{1,0:T(8,128)(2,1)S(1)}, bf16[32,512]{1,0:T(8,128)(2,1)S(1)}, u32[]{:S(2)}, u32[]{:S(2)}) collective-permute-start(bf16[32,512]{1,0:T(8,128)(2,1)S(1)} %get-tuple-element.364), channel_id=1, source_target_pairs={{1,0},{2,1},{3,2},{4,3},{5,4},{6,5},{7,6},{8,7},{9,8},{10,9},{11,1... | collective-permute-start | bytes 98312 | tf_op jit(solution)/shard_map/while/body/eval_jaxpr/ppermute | solution.py:20
  617.6 13.7 %collective-permute-start.2 = (bf16[32,512]{1,0:T(8,128)(2,1)S(1)}, bf16[32,512]{1,0:T(8,128)(2,1)S(1)}, u32[]{:S(2)}, u32[]{:S(2)}) collective-permute-start(bf16[32,512]{1,0:T(8,128)(2,1)S(1)} %get-tuple-element.368), channel_id=1, source_target_pairs={{1,0},{2,1},{3,2},{4,3},{5,4},{6,5},{7,6},{8,7},{9,8},{10,9},{11,1... | collective-permute-start | bytes 98312 | tf_op jit(solution)/shard_map/while/body/eval_jaxpr/ppermute | solution.py:20
  (83 other events, 670.7 us)
where the time goes:
time: 656 us; the launch traced here: 651 us
  starting transfers between devices  375 us (57%)
  waiting for transfers between devices  146 us (22%)
  matrix products  63.2 us (10%)
  other arithmetic  36.8 us (6%)
  local copies, waits for them, and re-layouts  25.5 us (4%)
    ppermute x38, starting transfers between devices, padded(): lax.ppermute(head, axis, [((i + 1) % count, i) for i in range(count)])  182 us
    ppermute x38, starting transfers between devices, passed_along(): return lax.ppermute(block, axis, route)  113 us
    ppermute x38, waiting for transfers between devices, passed_along(): return lax.ppermute(block, axis, route)  92.2 us
    ppermute x38, starting transfers between devices, padded(): lax.ppermute(tail, axis, [(i, (i + 1) % count) for i in range(count)])  79.2 us
    dot_general x38, matrix products, product(): jnp.einsum('mnb,nab->mna', picked, blocks, preferred_element_type=jnp.flo...  63.2 us
    ppermute x38, waiting for transfers between devices, padded(): lax.ppermute(tail, axis, [(i, (i + 1) % count) for i in range(count)])  53.5 us
    dynamic_update_slice x19, other arithmetic, finish(): lax.dynamic_update_slice_in_dim(stored, jnp.where(active, result, current...  30.1 us
    gather x38, local copies, waits for them, and re-layouts, product(): picked = jnp.take(tiles, local_cols, axis=1)  23.7 us
  transfers between devices with their start and end apart: 114, of which 38 were waited for; matrix products, arithmetic and copies ran while one was open for 9% of the time, Pallas kernels for 0%

commit v1 on v0

v1 whole, which is shorter than its diff:
```python
import functools

import jax
import jax.numpy as jnp
from jax import lax
from jax.experimental import pallas as pl
from jax.experimental.pallas import tpu as pltpu
from jax.sharding import PartitionSpec as P

HB = 4
MB = 4
MESH = pl.DeviceIdType.MESH


def sweep(
    slabs, laterals, kcount,
    thick_ref, layers_hbm, gdown_hbm, cdown_ref, gup_hbm, cup_ref,
    down_hbm, up_hbm,
    layers, green, source, ext, near, out,
    layer_sem, green_sem, recv_sem, send_sem, store_sem,
):
    depth, rows_all, width = layers.shape
    groups = ext.shape[1]
    rows = ext.shape[2]
    bsize = green.shape[-1]
    per_dev = width // bsize
    halo = HB * bsize
    slab = lax.axis_index("slab")
    cross = lax.axis_index("cross")
    right = lax.rem(cross + 1, laterals)
    left = lax.rem(cross + laterals - 1, laterals)
    last = slabs - 1

    def group_rows(m):
        return pl.ds(pl.multiple_of(m * rows, rows), rows)

    def layer_copy(m):
        part = group_rows(m)
        return pltpu.make_async_copy(
            layers_hbm.at[:, part, :], layers.at[:, part, :], layer_sem.at[m]
        )

    green_copies = [
        pltpu.make_async_copy(gdown_hbm.at[0], green.at[0], green_sem.at[0]),
        pltpu.make_async_copy(gup_hbm.at[0], green.at[1], green_sem.at[1]),
    ]
    for m in range(groups):
        layer_copy(m).start()
    for copy in green_copies:
        copy.start()

    barrier = pltpu.get_barrier_semaphore()
    for step, there in ((1, slab < last), (-1, slab > 0)):
        @pl.when(there)
        def _(step=step):
            for side in (left, cross, right):
                pl.semaphore_signal(
                    barrier, inc=1,
                    device_id={"slab": slab + step, "cross": side}, device_id_type=MESH,
                )
    pl.semaphore_wait(
        barrier, 3 * ((slab < last).astype(jnp.int32) + (slab > 0).astype(jnp.int32))
    )

    def sends(d, m):
        target = slab + 1 - 2 * d
        part = group_rows(m)
        pieces = (
            (0, halo, left, halo + width),
            (width - halo, halo, right, 0),
            (0, width, cross, halo),
        )
        return [
            pltpu.make_async_remote_copy(
                src_ref=out.at[d, part, pl.ds(at, size)],
                dst_ref=ext.at[d, m, :, pl.ds(to, size)],
                send_sem=send_sem.at[d, m, i],
                recv_sem=recv_sem.at[d, m, i],
                device_id={"slab": target, "cross": side},
                device_id_type=MESH,
            )
            for i, (at, size, side, to) in enumerate(pieces)
        ]

    def has_send(d):
        return slab != last * (1 - d)

    def store(d, m, ref):
        part = group_rows(m)
        return pltpu.make_async_copy(
            out.at[d, part, :], ref.at[0, part, :], store_sem.at[d, m]
        )

    def emit(d, m):
        @pl.when(has_send(d))
        def _():
            for copy in sends(d, m):
                copy.start()

        @pl.when(d == 0)
        def _():
            store(0, m, down_hbm).start()

        @pl.when(d == 1)
        def _():
            store(1, m, up_hbm).start()

    first = jnp.where(slab < slabs // 2, 0, 1)
    edge = jnp.logical_or(slab == 0, slab == last)

    @pl.loop(0, groups)
    def _(m):
        layer_copy(m).wait()
        part = group_rows(m)
        total = None
        for k in range(depth):
            keep = (k < thick_ref[0]).astype(jnp.float32)
            term = layers[k, part, :].astype(jnp.float32) * keep
            total = term if total is None else total + term
        source[part, :] = total

        @pl.when(edge)
        def _():
            out[first, part, :] = total.astype(out.dtype)
            emit(first, m)

    for copy in green_copies:
        copy.wait()

    def column(d, n):
        raw = jnp.where(d == 0, cdown_ref[0, n], cup_ref[0, n])
        return jnp.bitwise_and(raw - cross * per_dev + HB, near.shape[0] - 1)

    @pl.loop(jnp.where(edge, groups, 0), 2 * groups)
    def _(t):
        later = t // groups
        m = t - later * groups
        d = first + later - 2 * first * later
        for copy in sends(d, m):
            copy.wait_recv()
        part = group_rows(m)
        for blk in range(per_dev + 2 * HB):
            near[blk] = ext[d, m, :, blk * bsize:(blk + 1) * bsize]
        for b in range(per_dev):
            base = b * kcount
            picked = jnp.concatenate(
                [near[column(d, base + k)] for k in range(kcount)], axis=1
            )
            weights = jnp.concatenate(
                [green[d, base + k] for k in range(kcount)], axis=1
            )
            product = lax.dot_general(
                picked, weights, (((1,), (1,)), ((), ())),
                preferred_element_type=jnp.float32,
            )
            lanes = slice(b * bsize, (b + 1) * bsize)
            out[d, part, lanes] = (product + source[part, lanes]).astype(out.dtype)
        emit(d, m)

    for d, ref in ((0, down_hbm), (1, up_hbm)):
        @pl.when(has_send(d))
        def _(d=d):
            @pl.loop(0, groups)
            def _(m):
                for copy in sends(d, m):
                    copy.wait_send()

        @pl.loop(0, groups)
        def _(m, d=d, ref=ref):
            store(d, m, ref).wait()


def shards(slabs, laterals, thickness, layer_sources, green_down, column_down, green_up, column_up):
    depth, sources, width = layer_sources.shape
    blocks, bsize = green_down.shape[1], green_down.shape[-1]
    kcount = blocks // (width // bsize)
    rows = sources // MB
    extended = width + 2 * HB * bsize
    result = jax.ShapeDtypeStruct((1, sources, width), jnp.bfloat16)
    smem = pl.BlockSpec(memory_space=pltpu.SMEM)
    anywhere = pl.BlockSpec(memory_space=pl.ANY)
    return pl.pallas_call(
        functools.partial(sweep, slabs, laterals, kcount),
        out_shape=(result, result),
        in_specs=[smem, anywhere, anywhere, smem, anywhere, smem],
        out_specs=(anywhere, anywhere),
        scratch_shapes=[
            pltpu.VMEM((depth, sources, width), jnp.bfloat16),
            pltpu.VMEM((2, blocks, bsize, bsize), jnp.bfloat16),
            pltpu.VMEM((sources, width), jnp.float32),
            pltpu.VMEM((2, MB, rows, extended), jnp.bfloat16),
            pltpu.VMEM((extended // bsize, rows, bsize), jnp.bfloat16),
            pltpu.VMEM((2, sources, width), jnp.bfloat16),
            pltpu.SemaphoreType.DMA((MB,)),
            pltpu.SemaphoreType.DMA((2,)),
            pltpu.SemaphoreType.DMA((2, MB, 3)),
            pltpu.SemaphoreType.DMA((2, MB, 3)),
            pltpu.SemaphoreType.DMA((2, MB)),
        ],
        compiler_params=pltpu.CompilerParams(collective_id=0, has_side_effects=True),
    )(thickness, layer_sources, green_down, column_down, green_up, column_up)


def solution(mesh):
    return jax.shard_map(
        functools.partial(shards, mesh.shape["slab"], mesh.shape["cross"]),
        mesh=mesh,
        in_specs=(
            P("slab"),
            P("slab", None, "cross"),
            P("slab", "cross", None, None),
            P("slab", "cross"),
            P("slab", "cross", None, None),
            P("slab", "cross"),
        ),
        out_specs=(P("slab", None, "cross"), P("slab", None, "cross")),
        check_vma=False,
    )
```

time: 656 us -> 96.1 us (0.15)
  the two profiles are of different devices: /device:TPU:193 before, /device:TPU:30 now
where the time goes in v1:
time: 96.1 us; the launch traced here: 95.9 us
  Pallas kernels  91.2 us (95%)
  local copies, waits for them, and re-layouts  3.34 us (3%)
  between operations  1.28 us (1%)
    pallas_call x1, Pallas kernels, shards(): pl.pallas_call(functools.partial(sweep, slabs, laterals, kcount), out_sha...  91.2 us
    unnamed x2, local copies, waits for them, and re-layouts  3.34 us

profile of v1, /device:TPU:30, one launch (start us, length us, event | category | flops | bytes accessed | tf_op | source)
XLA Modules:
  0.0 95.9 jit_solution(11764288215058734096)
XLA Ops:
  1.3 91.2 %shard_map.77 = (bf16[1,128,1024]{2,1,0:T(8,128)(2,1)}, bf16[1,128,1024]{2,1,0:T(8,128)(2,1)}) custom-call(s32[1]{0:T(128)S(6)} %copy.10.thick_ref, bf16[4,128,1024]{2,1,0:T(8,128)(2,1)} %layers_hbm.1, bf16[1,48,128,128]{3,2,1,0:T(8,128)(2,1)} %gdown_hbm.1, s32[1,48]{1,0:T(1,128)} %cdown_ref.1, bf16[1,48,128,128]{3,2,1,0:T(8,128)(2,1)} %gup_hbm.1, ...), custom_call_target="tpu_custom_call" | custom-call | tf_op jit(solution)/shard_map/pallas_call | solution.py:182
  92.5 1.7 %copy.11 = bf16[1,128,1024]{2,1,0:T(8,128)(2,1)} copy(bf16[1,128,1024]{2,1,0:T(8,128)(2,1)} %get-tuple-element.4) | data formatting | bytes 524288
  94.2 1.7 %copy.12 = bf16[1,128,1024]{2,1,0:T(8,128)(2,1)} copy(bf16[1,128,1024]{2,1,0:T(8,128)(2,1)} %get-tuple-element.5) | data formatting | bytes 524288

commit v2 on v1

v2 whole, which is shorter than its diff:
```python
import functools

import jax
import jax.numpy as jnp
from jax import lax
from jax.experimental import pallas as pl
from jax.experimental.pallas import tpu as pltpu
from jax.sharding import PartitionSpec as P

HB = 4
MB = 4
ROW = 4
MESH = pl.DeviceIdType.MESH


def sweep(
    slabs, laterals, kcount,
    thick_ref, layers_hbm, gdown_hbm, cdown_ref, gup_hbm, cup_ref,
    down_hbm, up_hbm,
    layers, green, source, ext, near, out,
    layer_sem, green_sem, recv_sem, send_sem, store_sem,
):
    depth, _, width = layers.shape
    groups, rows = ext.shape[1], ext.shape[3]
    bsize = green.shape[-1]
    per_dev = width // bsize
    half = HB * bsize
    slab = lax.axis_index("slab")
    cross = lax.axis_index("cross")
    right = lax.rem(cross + 1, laterals)
    left = lax.rem(cross + laterals - 1, laterals)
    last = slabs - 1

    def group_rows(m):
        return pl.ds(pl.multiple_of(m * rows, rows), rows)

    def layer_copy(m):
        part = group_rows(m)
        return pltpu.make_async_copy(
            layers_hbm.at[:, part, :], layers.at[:, part, :], layer_sem.at[m]
        )

    green_copies = [
        pltpu.make_async_copy(gdown_hbm.at[0], green.at[0], green_sem.at[0]),
        pltpu.make_async_copy(gup_hbm.at[0], green.at[1], green_sem.at[1]),
    ]
    for m in range(groups):
        layer_copy(m).start()
    for copy in green_copies:
        copy.start()

    barrier = pltpu.get_barrier_semaphore()
    for step, there in ((1, slab < last), (-1, slab > 0)):
        @pl.when(there)
        def _(step=step):
            for side in (left, cross, right):
                pl.semaphore_signal(
                    barrier, inc=1,
                    device_id={"slab": slab + step, "cross": side}, device_id_type=MESH,
                )
    pl.semaphore_wait(
        barrier, 3 * ((slab < last).astype(jnp.int32) + (slab > 0).astype(jnp.int32))
    )

    def remote(d, m, h, piece, side):
        return pltpu.make_async_remote_copy(
            src_ref=out.at[d, h, group_rows(m), :],
            dst_ref=ext.at[d, m, piece],
            send_sem=send_sem.at[d, m, piece],
            recv_sem=recv_sem.at[d, m, piece],
            device_id={"slab": slab + 1 - 2 * d, "cross": side},
            device_id_type=MESH,
        )

    def sends(d, m, h):
        return [
            remote(d, m, h, 3 - 3 * h, left + h * (right - left)),
            remote(d, m, h, 1 + h, cross),
        ]

    def arrived(d, m, piece):
        remote(d, m, 0, piece, cross).wait_recv()

    def has_send(d):
        return slab != last * (1 - d)

    def store(d, m, h, ref):
        return pltpu.make_async_copy(
            out.at[d, h, group_rows(m), :],
            ref.at[0, group_rows(m), h * half:(h + 1) * half],
            store_sem.at[d, m, h],
        )

    def emit(d, m, h):
        @pl.when(has_send(d))
        def _():
            for copy in sends(d, m, h):
                copy.start()

    def keep(d, m):
        for want, ref in ((0, down_hbm), (1, up_hbm)):
            @pl.when(d == want)
            def _(want=want, ref=ref):
                for h in range(2):
                    store(want, m, h, ref).start()

    first = jnp.where(slab < slabs // 2, 0, 1)
    edge = jnp.logical_or(slab == 0, slab == last)
    lead = jnp.where(lax.rem(cross, ROW) == 0, 1, 0)

    @pl.loop(0, groups)
    def _(m):
        layer_copy(m).wait()
        part = group_rows(m)
        for h in range(2):
            total = None
            for k in range(depth):
                weight = (k < thick_ref[0]).astype(jnp.float32)
                term = layers[k, part, h * half:(h + 1) * half].astype(jnp.float32) * weight
                total = term if total is None else total + term
            source[h, part, :] = total

            @pl.when(edge)
            def _():
                out[first, h, part, :] = total.astype(out.dtype)
                emit(first, m, h)

        @pl.when(edge)
        def _():
            keep(first, m)

    for copy in green_copies:
        copy.wait()

    def flip(d):
        @pl.loop(0, green.shape[1], step=2)
        def _(i):
            for j in range(2):
                green[d, i + j] = green[d, i + j].T

    early = jnp.logical_and(slab >= slabs // 4, slab < slabs - slabs // 4)

    @pl.when(jnp.logical_not(edge))
    def _():
        flip(first)

    @pl.when(jnp.logical_or(early, edge))
    def _():
        flip(1 - first)

    def column(d, n):
        raw = jnp.where(d == 0, cdown_ref[0, n], cup_ref[0, n])
        return jnp.bitwise_and(raw - cross * per_dev + HB, near.shape[0] - 1)

    def bring(d, m, piece):
        arrived(d, m, piece)
        for j in range(HB):
            near[piece * HB + j] = ext[d, m, piece, :, j * bsize:(j + 1) * bsize]

    @pl.loop(jnp.where(edge, groups, 0), 2 * groups)
    def _(t):
        later = t // groups
        m = t - later * groups
        d = first + later - 2 * first * later
        part = group_rows(m)

        @pl.when(jnp.logical_and(t == groups, jnp.logical_not(jnp.logical_or(early, edge))))
        def _():
            flip(d)

        @pl.loop(0, 2)
        def _(i):
            h = lead + i - 2 * lead * i

            @pl.when(i == 0)
            def _():
                bring(d, m, 1)
                bring(d, m, 2)
                bring(d, m, 3 * h)

            @pl.when(i == 1)
            def _():
                bring(d, m, 3 * h)

            for b in range(HB):
                base = (h * HB + b) * kcount
                picked = jnp.concatenate(
                    [near[column(d, base + k)] for k in range(kcount)], axis=1
                )
                weights = green[d, pl.ds(base, kcount)].reshape(kcount * bsize, bsize)
                product = jnp.dot(picked, weights, preferred_element_type=jnp.float32)
                lanes = slice(b * bsize, (b + 1) * bsize)
                out[d, h, part, lanes] = (product + source[h, part, lanes]).astype(out.dtype)
            emit(d, m, h)

        keep(d, m)

    for d, ref in ((0, down_hbm), (1, up_hbm)):
        @pl.when(has_send(d))
        def _(d=d):
            @pl.loop(0, groups)
            def _(m):
                for h in range(2):
                    for copy in sends(d, m, h):
                        copy.wait_send()

        @pl.loop(0, groups)
        def _(m, d=d, ref=ref):
            for h in range(2):
                store(d, m, h, ref).wait()


def shards(slabs, laterals, thickness, layer_sources, green_down, column_down, green_up, column_up):
    depth, sources, width = layer_sources.shape
    blocks, bsize = green_down.shape[1], green_down.shape[-1]
    kcount = blocks // (width // bsize)
    rows = sources // MB
    half = HB * bsize
    result = jax.ShapeDtypeStruct((1, sources, width), jnp.bfloat16)
    smem = pl.BlockSpec(memory_space=pltpu.SMEM)
    anywhere = pl.BlockSpec(memory_space=pl.ANY)
    layer_sources, green_down, column_down, green_up, column_up = (
        pltpu.with_memory_space_constraint(array, pltpu.HBM)
        for array in (layer_sources, green_down, column_down, green_up, column_up)
    )
    return pl.pallas_call(
        functools.partial(sweep, slabs, laterals, kcount),
        out_shape=(result, result),
        in_specs=[smem, anywhere, anywhere, smem, anywhere, smem],
        out_specs=(anywhere, anywhere),
        scratch_shapes=[
            pltpu.VMEM((depth, sources, width), jnp.bfloat16),
            pltpu.VMEM((2, blocks, bsize, bsize), jnp.bfloat16),
            pltpu.VMEM((2, sources, half), jnp.float32),
            pltpu.VMEM((2, MB, 4, rows, half), jnp.bfloat16),
            pltpu.VMEM((4 * HB, rows, bsize), jnp.bfloat16),
            pltpu.VMEM((2, 2, sources, half), jnp.bfloat16),
            pltpu.SemaphoreType.DMA((MB,)),
            pltpu.SemaphoreType.DMA((2,)),
            pltpu.SemaphoreType.DMA((2, MB, 4)),
            pltpu.SemaphoreType.DMA((2, MB, 4)),
            pltpu.SemaphoreType.DMA((2, MB, 2)),
        ],
        compiler_params=pltpu.CompilerParams(
            collective_id=0, has_side_effects=True, vmem_limit_bytes=12 << 20
        ),
    )(thickness, layer_sources, green_down, column_down, green_up, column_up)


def solution(mesh):
    return jax.shard_map(
        functools.partial(shards, mesh.shape["slab"], mesh.shape["cross"]),
        mesh=mesh,
        in_specs=(
            P("slab"),
            P("slab", None, "cross"),
            P("slab", "cross", None, None),
            P("slab", "cross"),
            P("slab", "cross", None, None),
            P("slab", "cross"),
        ),
        out_specs=(P("slab", None, "cross"), P("slab", None, "cross")),
        check_vma=False,
    )
```

time: 96.1 us -> 87.4 us (0.909)
  the two profiles are of different devices: /device:TPU:30 before, /device:TPU:2 now
where the time goes in v2:
time: 87.4 us; the launch traced here: 87.3 us
  Pallas kernels  84.6 us (97%)
  local copies, waits for them, and re-layouts  1.41 us (2%)
  between operations  1.28 us (1%)
    pallas_call x1, Pallas kernels, shards(): pl.pallas_call(functools.partial(sweep, slabs, laterals, kcount), out_sha...  84.6 us

profile of v2, /device:TPU:2, one launch (start us, length us, event | category | flops | bytes accessed | tf_op | source)
XLA Modules:
  0.0 87.3 jit_solution(14438347456926919142)
XLA Ops:
  1.3 84.6 %shard_map.77 = (bf16[1,128,1024]{2,1,0:T(8,128)(2,1)S(1)}, bf16[1,128,1024]{2,1,0:T(8,128)(2,1)S(1)}) custom-call(s32[1]{0:T(128)S(6)} %copy.10.thick_ref, bf16[4,128,1024]{2,1,0:T(8,128)(2,1)} %layers_hbm.1, bf16[1,48,128,128]{3,2,1,0:T(8,128)(2,1)} %gdown_hbm.1, s32[1,48]{1,0:T(1,128)} %cdown_ref.1, bf16[1,48,128,128]{3,2,1,0:T(8,128)(2,1)} %gup_hbm.1, ...), custom_call_target="tpu_custom_call" | custom-call | tf_op jit(solution)/shard_map/pallas_call | solution.py:226
  85.9 0.7 copy.11
  86.6 0.7 copy.12

commit v3 on v2

--- a/solution.py
+++ b/solution.py
@@ -10,15 +10,16 @@
 HB = 4
 MB = 4
 ROW = 4
+START = 4
 MESH = pl.DeviceIdType.MESH
 
 
 def sweep(
     slabs, laterals, kcount,
-    thick_ref, layers_hbm, gdown_hbm, cdown_ref, gup_hbm, cup_ref,
+    thick_ref, layers_hbm, gdown_hbm, cdown_ref, gup_hbm, cup_ref, cdown_hbm, cup_hbm,
     down_hbm, up_hbm,
-    layers, green, source, ext, near, out,
-    layer_sem, green_sem, recv_sem, send_sem, store_sem,
+    layers, green, source, ext, near, out, far_green, far_column, far_source, far_out,
+    layer_sem, green_sem, recv_sem, send_sem, store_sem, far_recv, far_send,
 ):
     depth, _, width = layers.shape
     groups, rows = ext.shape[1], ext.shape[3]
@@ -30,6 +31,13 @@
     right = lax.rem(cross + 1, laterals)
     left = lax.rem(cross + laterals - 1, laterals)
     last = slabs - 1
+    at = lax.rem(cross, ROW)
+    border = jnp.logical_or(at == 0, at == ROW - 1)
+    hx = jnp.where(at == 0, 0, 1)
+    across = left + hx * (right - left)
+    dx = lax.rem(slab, 2)
+    inner = slab + dx * (last - 2 * slab) >= START
+    helps = jnp.logical_and(border, inner)
 
     def group_rows(m):
         return pl.ds(pl.multiple_of(m * rows, rows), rows)
@@ -58,28 +66,79 @@
                     barrier, inc=1,
                     device_id={"slab": slab + step, "cross": side}, device_id_type=MESH,
                 )
+    @pl.when(helps)
+    def _():
+        pl.semaphore_signal(
+            barrier, inc=1, device_id={"slab": slab, "cross": across}, device_id_type=MESH
+        )
     pl.semaphore_wait(
-        barrier, 3 * ((slab < last).astype(jnp.int32) + (slab > 0).astype(jnp.int32))
+        barrier,
+        3 * ((slab < last).astype(jnp.int32) + (slab > 0).astype(jnp.int32))
+        + helps.astype(jnp.int32),
     )
 
-    def remote(d, m, h, piece, side):
+    def place(d):
+        return slab + d * (last - 2 * slab)
+
+    def even(d):
+        return jnp.logical_and(lax.rem(place(d), 2) == 0, place(d) >= START)
+
+    def remote(d, m, src, piece, side, slot):
         return pltpu.make_async_remote_copy(
-            src_ref=out.at[d, h, group_rows(m), :],
+            src_ref=src,
             dst_ref=ext.at[d, m, piece],
-            send_sem=send_sem.at[d, m, piece],
+            send_sem=send_sem.at[d, m, slot],
             recv_sem=recv_sem.at[d, m, piece],
             device_id={"slab": slab + 1 - 2 * d, "cross": side},
             device_id_type=MESH,
         )
 
-    def sends(d, m, h):
-        return [
-            remote(d, m, h, 3 - 3 * h, left + h * (right - left)),
-            remote(d, m, h, 1 + h, cross),
-        ]
+    def own_half(d, m, h):
+        return out.at[d, h, group_rows(m), :]
+
+    def sends(d, m, h, act):
+        crossing = jnp.logical_and(border, h == hx)
+
+        @pl.when(jnp.logical_not(jnp.logical_and(crossing, even(d))))
+        def _():
+            act(remote(d, m, own_half(d, m, h), 3 - 3 * h, left + h * (right - left), 3 - 3 * h))
+        act(remote(d, m, own_half(d, m, h), 1 + h, cross, 1 + h))
+
+        @pl.when(
+            jnp.logical_and(
+                jnp.logical_and(border, h != hx),
+                jnp.logical_and(lax.rem(place(d), 2) == 1, place(d) >= START - 1),
+            )
+        )
+        def _():
+            act(remote(d, m, own_half(d, m, h), 4, across, 4))
+
+    def far_send_out(d, m, act):
+        act(remote(d, m, far_out.at[m], 3 * hx, cross, 5))
+
+    def over(src, dst, i):
+        return pltpu.make_async_remote_copy(
+            src_ref=src, dst_ref=dst, send_sem=far_send.at[i], recv_sem=far_recv.at[i],
+            device_id={"slab": slab, "cross": across}, device_id_type=MESH,
+        )
+
+    per_half = HB * kcount
+
+    def over_green(ref):
+        return over(ref.at[0, pl.ds(hx * per_half, per_half)], far_green, 0)
+
+    def over_source(m):
+        return over(source.at[hx, group_rows(m), :], far_source.at[group_rows(m), :], 2 + m)
+
+    def hand_over_green():
+        for want, gref, cref in ((0, gdown_hbm, cdown_hbm), (1, gup_hbm, cup_hbm)):
+            @pl.when(dx == want)
+            def _(gref=gref, cref=cref):
+                over(cref, far_column, 1).start()
+                over_green(gref).start()
 
     def arrived(d, m, piece):
-        remote(d, m, 0, piece, cross).wait_recv()
+        remote(d, m, own_half(d, m, 0), piece, cross, piece).wait_recv()
 
     def has_send(d):
         return slab != last * (1 - d)
@@ -94,8 +153,7 @@
     def emit(d, m, h):
         @pl.when(has_send(d))
         def _():
-            for copy in sends(d, m, h):
-                copy.start()
+            sends(d, m, h, lambda copy: copy.start())
 
     def keep(d, m):
         for want, ref in ((0, down_hbm), (1, up_hbm)):
@@ -106,7 +164,13 @@
 
     first = jnp.where(slab < slabs // 2, 0, 1)
     edge = jnp.logical_or(slab == 0, slab == last)
-    lead = jnp.where(lax.rem(cross, ROW) == 0, 1, 0)
+    lead = jnp.where(at == 0, 1, 0)
+    middle = jnp.logical_or(slab == slabs // 2, slab == slabs // 2 - 1)
+    soon = jnp.logical_or(dx == first, middle)
+
+    @pl.when(jnp.logical_and(helps, soon))
+    def _():
+        hand_over_green()
 
     @pl.loop(0, groups)
     def _(m):
@@ -129,6 +193,10 @@
         def _():
             keep(first, m)
 
+        @pl.when(jnp.logical_and(helps, soon))
+        def _():
+            over_source(m).start()
+
     for copy in green_copies:
         copy.wait()
 
@@ -148,14 +216,16 @@
     def _():
         flip(1 - first)
 
+    def slot_of(raw):
+        return jnp.bitwise_and(raw - cross * per_dev + 3 * HB, near.shape[0] - 1)
+
     def column(d, n):
-        raw = jnp.where(d == 0, cdown_ref[0, n], cup_ref[0, n])
-        return jnp.bitwise_and(raw - cross * per_dev + HB, near.shape[0] - 1)
-
-    def bring(d, m, piece):
+        return slot_of(jnp.where(d == 0, cdown_ref[0, n], cup_ref[0, n]))
+
+    def bring(d, m, piece, base):
         arrived(d, m, piece)
         for j in range(HB):
-            near[piece * HB + j] = ext[d, m, piece, :, j * bsize:(j + 1) * bsize]
+            near[base + j] = ext[d, m, piece, :, j * bsize:(j + 1) * bsize]
 
     @pl.loop(jnp.where(edge, groups, 0), 2 * groups)
     def _(t):
@@ -168,19 +238,26 @@
         def _():
             flip(d)
 
+        @pl.when(
+            jnp.logical_and(
+                t == groups, jnp.logical_and(helps, jnp.logical_not(soon))
+            )
+        )
+        def _():
+            hand_over_green()
+            for j in range(groups):
+                over_source(j).start()
+
         @pl.loop(0, 2)
         def _(i):
             h = lead + i - 2 * lead * i
 
             @pl.when(i == 0)
             def _():
-                bring(d, m, 1)
-                bring(d, m, 2)
-                bring(d, m, 3 * h)
-
-            @pl.when(i == 1)
-            def _():
-                bring(d, m, 3 * h)
+                bring(d, m, 1, 3 * HB)
+                bring(d, m, 2, 4 * HB)
+
+            bring(d, m, 3 * h, (2 + 3 * h) * HB)
 
             for b in range(HB):
                 base = (h * HB + b) * kcount
@@ -193,7 +270,40 @@
                 out[d, h, part, lanes] = (product + source[h, part, lanes]).astype(out.dtype)
             emit(d, m, h)
 
+        @pl.when(jnp.logical_and(border, even(d)))
+        def _():
+            @pl.when(m == 0)
+            def _():
+                over(cdown_hbm, far_column, 1).wait_recv()
+                over_green(gdown_hbm).wait_recv()
+            over_source(m).wait_recv()
+            bring(d, m, 4, (1 + 5 * hx) * HB)
+            for b in range(HB):
+                base = b * kcount
+                picked = jnp.concatenate(
+                    [
+                        near[slot_of(far_column[0, (1 - hx) * per_half + base + k])]
+                        for k in range(kcount)
+                    ],
+                    axis=1,
+                )
+                weights = jnp.concatenate([far_green[base + k] for k in range(kcount)], axis=1)
+                product = lax.dot_general(
+                    picked, weights, (((1,), (1,)), ((), ())),
+                    preferred_element_type=jnp.float32,
+                )
+                lanes = slice(b * bsize, (b + 1) * bsize)
+                far_out[m, :, lanes] = (product + far_source[part, lanes]).astype(far_out.dtype)
+            far_send_out(d, m, lambda copy: copy.start())
+
         keep(d, m)
+
+    @pl.when(helps)
+    def _():
+        over(cdown_hbm, far_column, 1).wait_send()
+        over_green(gdown_hbm).wait_send()
+        for j in range(groups):
+            over_source(j).wait_send()
 
     for d, ref in ((0, down_hbm), (1, up_hbm)):
         @pl.when(has_send(d))
@@ -201,8 +311,11 @@
             @pl.loop(0, groups)
             def _(m):
                 for h in range(2):
-                    for copy in sends(d, m, h):
-                        copy.wait_send()
+                    sends(d, m, h, lambda copy: copy.wait_send())
+
+                @pl.when(jnp.logical_and(border, even(d)))
+                def _():
+                    far_send_out(d, m, lambda copy: copy.wait_send())
 
         @pl.loop(0, groups)
         def _(m, d=d, ref=ref):
@@ -226,25 +339,34 @@
     return pl.pallas_call(
         functools.partial(sweep, slabs, laterals, kcount),
         out_shape=(result, result),
-        in_specs=[smem, anywhere, anywhere, smem, anywhere, smem],
+        in_specs=[smem, anywhere, anywhere, smem, anywhere, smem, anywhere, anywhere],
         out_specs=(anywhere, anywhere),
         scratch_shapes=[
             pltpu.VMEM((depth, sources, width), jnp.bfloat16),
             pltpu.VMEM((2, blocks, bsize, bsize), jnp.bfloat16),
             pltpu.VMEM((2, sources, half), jnp.float32),
-            pltpu.VMEM((2, MB, 4, rows, half), jnp.bfloat16),
-            pltpu.VMEM((4 * HB, rows, bsize), jnp.bfloat16),
+            pltpu.VMEM((2, MB, 5, rows, half), jnp.bfloat16),
+            pltpu.VMEM((8 * HB, rows, bsize), jnp.bfloat16),
             pltpu.VMEM((2, 2, sources, half), jnp.bfloat16),
+            pltpu.VMEM((HB * kcount, bsize, bsize), jnp.bfloat16),
+            pltpu.SMEM((1, blocks), jnp.int32),
+            pltpu.VMEM((sources, half), jnp.float32),
+            pltpu.VMEM((MB, rows, half), jnp.bfloat16),
             pltpu.SemaphoreType.DMA((MB,)),
             pltpu.SemaphoreType.DMA((2,)),
-            pltpu.SemaphoreType.DMA((2, MB, 4)),
-            pltpu.SemaphoreType.DMA((2, MB, 4)),
+            pltpu.SemaphoreType.DMA((2, MB, 5)),
+            pltpu.SemaphoreType.DMA((2, MB, 6)),
             pltpu.SemaphoreType.DMA((2, MB, 2)),
+            pltpu.SemaphoreType.DMA((2 + MB,)),
+            pltpu.SemaphoreType.DMA((2 + MB,)),
         ],
         compiler_params=pltpu.CompilerParams(
             collective_id=0, has_side_effects=True, vmem_limit_bytes=12 << 20
         ),
-    )(thickness, layer_sources, green_down, column_down, green_up, column_up)
+    )(
+        thickness, layer_sources, green_down, column_down, green_up, column_up,
+        column_down, column_up,
+    )
 
 
 def solution(mesh):

time: 87.4 us -> 79.6 us (0.911)
  Pallas kernels: 84.6 us -> 76.8 us
    pallas_call x1, Pallas kernels: 84.6 us -> 76.8 us  [shards(): pl.pallas_call(functools.partial(sweep, slabs, laterals, kcount), out_sha...]
where the time goes in v3:
time: 79.6 us; the launch traced here: 79.5 us
  Pallas kernels  76.8 us (96%)
  local copies, waits for them, and re-layouts  1.41 us (2%)
  between operations  1.28 us (2%)
    pallas_call x1, Pallas kernels, shards(): pl.pallas_call(functools.partial(sweep, slabs, laterals, kcount), out_sha...  76.8 us

profile of v3, /device:TPU:2, one launch (start us, length us, event | category | flops | bytes accessed | tf_op | source)
XLA Modules:
  0.0 79.5 jit_solution(17567640318894390725)
XLA Ops:
  1.3 76.8 %shard_map.77 = (bf16[1,128,1024]{2,1,0:T(8,128)(2,1)S(1)}, bf16[1,128,1024]{2,1,0:T(8,128)(2,1)S(1)}) custom-call(s32[1]{0:T(128)S(6)} %copy.10.thick_ref, bf16[4,128,1024]{2,1,0:T(8,128)(2,1)} %layers_hbm.1, bf16[1,48,128,128]{3,2,1,0:T(8,128)(2,1)} %gdown_hbm.1, s32[1,48]{1,0:T(1,128)} %cdown_hbm.1, bf16[1,48,128,128]{3,2,1,0:T(8,128)(2,1)} %gup_hbm.1, ...), custom_call_target="tpu_custom_call" | custom-call | tf_op jit(solution)/shard_map/pallas_call | solution.py:339
  78.0 0.7 copy.11
  78.7 0.7 copy.12

commit v4 on v3

--- a/solution.py
+++ b/solution.py
@@ -8,7 +8,7 @@
 from jax.sharding import PartitionSpec as P
 
 HB = 4
-MB = 4
+MB = 8
 ROW = 4
 START = 4
 MESH = pl.DeviceIdType.MESH
@@ -16,10 +16,10 @@
 
 def sweep(
     slabs, laterals, kcount,
-    thick_ref, layers_hbm, gdown_hbm, cdown_ref, gup_hbm, cup_ref, cdown_hbm, cup_hbm,
+    thick_hbm, layers_hbm, gdown_hbm, cdown_hbm, gup_hbm, cup_hbm,
     down_hbm, up_hbm,
-    layers, green, source, ext, near, out, far_green, far_column, far_source, far_out,
-    layer_sem, green_sem, recv_sem, send_sem, store_sem, far_recv, far_send,
+    thick_ref, cdown_ref, cup_ref, layers, green, source, ext, near, out, far_green, far_column, far_source, far_out,
+    layer_sem, green_sem, recv_sem, send_sem, store_sem, far_recv, far_send, small_sem,
 ):
     depth, _, width = layers.shape
     groups, rows = ext.shape[1], ext.shape[3]
@@ -52,8 +52,16 @@
         pltpu.make_async_copy(gdown_hbm.at[0], green.at[0], green_sem.at[0]),
         pltpu.make_async_copy(gup_hbm.at[0], green.at[1], green_sem.at[1]),
     ]
+    thick_copy = pltpu.make_async_copy(thick_hbm, thick_ref, small_sem.at[0])
+    column_copies = [
+        pltpu.make_async_copy(cdown_hbm, cdown_ref, small_sem.at[1]),
+        pltpu.make_async_copy(cup_hbm, cup_ref, small_sem.at[2]),
+    ]
+    thick_copy.start()
     for m in range(groups):
         layer_copy(m).start()
+    for copy in column_copies:
+        copy.start()
     for copy in green_copies:
         copy.start()
 
@@ -171,6 +179,8 @@
     @pl.when(jnp.logical_and(helps, soon))
     def _():
         hand_over_green()
+
+    thick_copy.wait()
 
     @pl.loop(0, groups)
     def _(m):
@@ -197,7 +207,7 @@
         def _():
             over_source(m).start()
 
-    for copy in green_copies:
+    for copy in column_copies + green_copies:
         copy.wait()
 
     def flip(d):
@@ -215,6 +225,19 @@
     @pl.when(jnp.logical_or(early, edge))
     def _():
         flip(1 - first)
+
+    def take_far_green():
+        over(cdown_hbm, far_column, 1).wait_recv()
+        over_green(gdown_hbm).wait_recv()
+
+        @pl.loop(0, far_green.shape[0], step=2)
+        def _(i):
+            for j in range(2):
+                far_green[i + j] = far_green[i + j].T
+
+    @pl.when(jnp.logical_and(helps, soon))
+    def _():
+        take_far_green()
 
     def slot_of(raw):
         return jnp.bitwise_and(raw - cross * per_dev + 3 * HB, near.shape[0] - 1)
@@ -247,6 +270,7 @@
             hand_over_green()
             for j in range(groups):
                 over_source(j).start()
+            take_far_green()
 
         @pl.loop(0, 2)
         def _(i):
@@ -272,10 +296,6 @@
 
         @pl.when(jnp.logical_and(border, even(d)))
         def _():
-            @pl.when(m == 0)
-            def _():
-                over(cdown_hbm, far_column, 1).wait_recv()
-                over_green(gdown_hbm).wait_recv()
             over_source(m).wait_recv()
             bring(d, m, 4, (1 + 5 * hx) * HB)
             for b in range(HB):
@@ -287,11 +307,8 @@
                     ],
                     axis=1,
                 )
-                weights = jnp.concatenate([far_green[base + k] for k in range(kcount)], axis=1)
-                product = lax.dot_general(
-                    picked, weights, (((1,), (1,)), ((), ())),
-                    preferred_element_type=jnp.float32,
-                )
+                weights = far_green[base:base + kcount].reshape(kcount * bsize, bsize)
+                product = jnp.dot(picked, weights, preferred_element_type=jnp.float32)
                 lanes = slice(b * bsize, (b + 1) * bsize)
                 far_out[m, :, lanes] = (product + far_source[part, lanes]).astype(far_out.dtype)
             far_send_out(d, m, lambda copy: copy.start())
@@ -323,6 +340,17 @@
                 store(d, m, h, ref).wait()
 
 
+def put_out(down_ref, up_ref, down_out, up_out, sem):
+    copies = [
+        pltpu.make_async_copy(down_ref, down_out, sem.at[0]),
+        pltpu.make_async_copy(up_ref, up_out, sem.at[1]),
+    ]
+    for copy in copies:
+        copy.start()
+    for copy in copies:
+        copy.wait()
+
+
 def shards(slabs, laterals, thickness, layer_sources, green_down, column_down, green_up, column_up):
     depth, sources, width = layer_sources.shape
     blocks, bsize = green_down.shape[1], green_down.shape[-1]
@@ -330,18 +358,18 @@
     rows = sources // MB
     half = HB * bsize
     result = jax.ShapeDtypeStruct((1, sources, width), jnp.bfloat16)
-    smem = pl.BlockSpec(memory_space=pltpu.SMEM)
     anywhere = pl.BlockSpec(memory_space=pl.ANY)
-    layer_sources, green_down, column_down, green_up, column_up = (
-        pltpu.with_memory_space_constraint(array, pltpu.HBM)
-        for array in (layer_sources, green_down, column_down, green_up, column_up)
-    )
-    return pl.pallas_call(
+    given = (layer_sources, green_down, column_down, green_up, column_up)
+    given = [pltpu.with_memory_space_constraint(array, pltpu.HBM) for array in given]
+    traces = pl.pallas_call(
         functools.partial(sweep, slabs, laterals, kcount),
         out_shape=(result, result),
-        in_specs=[smem, anywhere, anywhere, smem, anywhere, smem, anywhere, anywhere],
+        in_specs=[anywhere] * 6,
         out_specs=(anywhere, anywhere),
         scratch_shapes=[
+            pltpu.SMEM((1,), jnp.int32),
+            pltpu.SMEM((1, blocks), jnp.int32),
+            pltpu.SMEM((1, blocks), jnp.int32),
             pltpu.VMEM((depth, sources, width), jnp.bfloat16),
             pltpu.VMEM((2, blocks, bsize, bsize), jnp.bfloat16),
             pltpu.VMEM((2, sources, half), jnp.float32),
@@ -359,14 +387,20 @@
             pltpu.SemaphoreType.DMA((2, MB, 2)),
             pltpu.SemaphoreType.DMA((2 + MB,)),
             pltpu.SemaphoreType.DMA((2 + MB,)),
+            pltpu.SemaphoreType.DMA((3,)),
         ],
         compiler_params=pltpu.CompilerParams(
             collective_id=0, has_side_effects=True, vmem_limit_bytes=12 << 20
         ),
-    )(
-        thickness, layer_sources, green_down, column_down, green_up, column_up,
-        column_down, column_up,
-    )
+    )(thickness, *given)
+    return pl.pallas_call(
+        put_out,
+        out_shape=(result, result),
+        in_specs=[anywhere] * 2,
+        out_specs=(anywhere, anywhere),
+        scratch_shapes=[pltpu.SemaphoreType.DMA((2,))],
+        compiler_params=pltpu.CompilerParams(vmem_limit_bytes=1 << 20),
+    )(*traces)
 
 
 def solution(mesh):

time: 79.6 us -> 76.8 us (0.965)
  local copies, waits for them, and re-layouts: 1.41 us -> 0 us
  Pallas kernels: 76.8 us -> 75.4 us
    pallas_call x1, Pallas kernels: 76.8 us -> 74.6 us  [shards(): pl.pallas_call(functools.partial(sweep, slabs, laterals, kcount), out_sha...]
    unnamed x2 -> x0, local copies, waits for them, and re-layouts: 1.41 us -> none
    pallas_call x0 -> x1, Pallas kernels: none -> 0.81 us  [shards(): pl.pallas_call(put_out, out_shape=(result, result), in_specs=[anywhere] *...]
where the time goes in v4:
time: 76.8 us; the launch traced here: 76.7 us
  Pallas kernels  75.4 us (98%)
  between operations  1.28 us (2%)
    pallas_call x1, Pallas kernels, shards(): pl.pallas_call(functools.partial(sweep, slabs, laterals, kcount), out_sha...  74.6 us

profile of v4, /device:TPU:2, one launch (start us, length us, event | category | flops | bytes accessed | tf_op | source)
XLA Modules:
  0.0 76.7 jit_solution(8782358856549111008)
XLA Ops:
  1.3 74.6 %shard_map.77 = (bf16[1,128,1024]{2,1,0:T(8,128)(2,1)S(1)}, bf16[1,128,1024]{2,1,0:T(8,128)(2,1)S(1)}) custom-call(s32[1]{0:T(128)S(6)} %copy.8.thick_hbm, bf16[4,128,1024]{2,1,0:T(8,128)(2,1)} %layers_hbm.1, bf16[1,48,128,128]{3,2,1,0:T(8,128)(2,1)} %gdown_hbm.1, s32[1,48]{1,0:T(1,128)} %cdown_hbm.1, bf16[1,48,128,128]{3,2,1,0:T(8,128)(2,1)} %gup_hbm.1, ...), custom_call_target="tpu_custom_call" | custom-call | tf_op jit(solution)/shard_map/pallas_call | solution.py:364
  75.9 0.8 %shard_map.78 = (bf16[1,128,1024]{2,1,0:T(8,128)(2,1)}, bf16[1,128,1024]{2,1,0:T(8,128)(2,1)}) custom-call(bf16[1,128,1024]{2,1,0:T(8,128)(2,1)S(1)} %get-tuple-element.4.down_ref, bf16[1,128,1024]{2,1,0:T(8,128)(2,1)S(1)} %get-tuple-element.5.up_ref), custom_call_target="tpu_custom_call" | custom-call | tf_op jit(solution)/shard_map/pallas_call | solution.py:396

commit v5 on v4

--- a/solution.py
+++ b/solution.py
@@ -272,7 +272,7 @@
                 over_source(j).start()
             take_far_green()
 
-        @pl.loop(0, 2)
+        @pl.loop(0, 2, unroll=True)
         def _(i):
             h = lead + i - 2 * lead * i
 

time: 76.8 us -> 76.5 us (level)
  no operation moved by 1% of the time
where the time goes in v5:
time: 76.5 us; the launch traced here: 76.4 us
  Pallas kernels  75.1 us (98%)
  between operations  1.28 us (2%)
    pallas_call x1, Pallas kernels, shards(): pl.pallas_call(functools.partial(sweep, slabs, laterals, kcount), out_sha...  74.3 us

profile of v5, /device:TPU:2, one launch (start us, length us, event | category | flops | bytes accessed | tf_op | source)
XLA Modules:
  0.0 76.4 jit_solution(16101072751725943963)
XLA Ops:
  1.3 74.3 %shard_map.77 = (bf16[1,128,1024]{2,1,0:T(8,128)(2,1)S(1)}, bf16[1,128,1024]{2,1,0:T(8,128)(2,1)S(1)}) custom-call(s32[1]{0:T(128)S(6)} %copy.8.thick_hbm, bf16[4,128,1024]{2,1,0:T(8,128)(2,1)} %layers_hbm.1, bf16[1,48,128,128]{3,2,1,0:T(8,128)(2,1)} %gdown_hbm.1, s32[1,48]{1,0:T(1,128)} %cdown_hbm.1, bf16[1,48,128,128]{3,2,1,0:T(8,128)(2,1)} %gup_hbm.1, ...), custom_call_target="tpu_custom_call" | custom-call | tf_op jit(solution)/shard_map/pallas_call | solution.py:364
  75.5 0.8 %shard_map.78 = (bf16[1,128,1024]{2,1,0:T(8,128)(2,1)}, bf16[1,128,1024]{2,1,0:T(8,128)(2,1)}) custom-call(bf16[1,128,1024]{2,1,0:T(8,128)(2,1)S(1)} %get-tuple-element.4.down_ref, bf16[1,128,1024]{2,1,0:T(8,128)(2,1)S(1)} %get-tuple-element.5.up_ref), custom_call_target="tpu_custom_call" | custom-call | tf_op jit(solution)/shard_map/pallas_call | solution.py:396
